TPU v7x, 512 devices: a whole 4x4x16 slice. The times are simulated.
512 devices in a mesh: dp: 64 (over z, y), section: 2 (over core), mp: 4 (over x).
Axes of the slice: x: 4, y: 4, z: 16, core: 2. Of those that a mesh axis runs over, the one named last changes fastest.
Arguments:
- frames: bfloat16 [64, 128, 512], P('dp'), may hold values from -6 to 6
- lengths: int32 [64], P('dp'), may hold values from 32 to 128
- feature_proj: bfloat16 [512, 1920], P(None, 'mp'), may hold values from -0.25 to 0.25
- norm_gain: float32 [2, 1920], P('section'), may hold values from 0.25 to 1.75
- qkv_weight: bfloat16 [2, 1920, 5760], P('section', 'dp', 'mp'), may hold values from -0.125 to 0.125
- out_weight: bfloat16 [2, 1920, 1920], P('section', 'mp', 'dp'), may hold values from -0.125 to 0.125
- center: float32 [1920], replicated, may hold values from -4 to 4
- whitening: float32 [1920, 1024], P(None, 'dp'), may hold values from -0.125 to 0.125
Outputs:
- embeddings: float32 [64, 1024], P(None, 'dp')
All inputs are finite; a program needn't handle non-finite values.
Results may differ from a plain program's by a relative error of at most 0.0095.
Values may be sent and summed in bfloat16 or wider, within the bound.
No kernel may reach another device: no remote copies, remote signals or barrier semaphores. Data moves between devices by JAX's collectives and lax.ppermute only.
A program may use at most 64 MiB of HBM per device.

v0:
```python
import jax
import jax.numpy as jnp
from jax import lax
from jax.sharding import PartitionSpec as P

HD = 120


def passed_along(x, axis, by):
    count = lax.axis_size(axis)
    pairs = [(i, i + by) for i in range(count) if 0 <= i + by < count]
    return lax.ppermute(x, axis, pairs)


def broadcast(value, axis, source):
    kept = jnp.where(lax.axis_index(axis) == source, value, 0).astype(value.dtype)
    return lax.psum(kept, axis)


def layer_norm(values, gain):
    mean = jnp.mean(values, axis=-1, keepdims=True)
    centered = values - mean
    var = jnp.mean(centered * centered, axis=-1, keepdims=True)
    return centered * lax.rsqrt(var + 1e-05) * gain


def body(frames, lengths, feature_proj, norm_gain, qkv_weight, out_weight, center, whitening):
    section_index = lax.axis_index("section")
    gain = norm_gain[0]
    qkv_local = qkv_weight[0]
    out_local = out_weight[0]
    count_utt = frames.shape[0]
    frames_count = frames.shape[1]
    width = gain.shape[0]
    qkv_cols = qkv_local.shape[1]
    heads_local = qkv_cols // (3 * HD)
    full_qkv, full_out = (
        lax.all_gather(qkv_local, "dp", axis=0, tiled=True),
        lax.all_gather(out_local, "dp", axis=1, tiled=True),
    )
    received = jnp.zeros((frames_count, width), jnp.bfloat16)
    pooled_rows = []
    frame_ids = jnp.arange(frames_count, dtype=jnp.int32)
    for step in range(count_utt + 1):
        first_mb = min(step, count_utt - 1)
        second_mb = max(step - 1, 0)
        projected_part = jnp.dot(
            frames[first_mb], feature_proj, preferred_element_type=jnp.float32
        ).astype(jnp.bfloat16)
        projected = lax.all_gather(projected_part, "mp", axis=1, tiled=True)
        first_section = section_index == 0
        layer_input = jnp.where(first_section, projected, received)
        length = jnp.where(first_section, lengths[first_mb], lengths[second_mb])
        normed = layer_norm(layer_input.astype(jnp.float32), gain).astype(jnp.bfloat16)
        qkv_sum = jnp.dot(normed, full_qkv, preferred_element_type=jnp.float32)
        qkv = qkv_sum.astype(jnp.bfloat16).reshape(frames_count, 3, heads_local, HD)
        query = qkv[:, 0]
        keys = qkv[:, 1]
        values = qkv[:, 2]
        scores = jnp.einsum(
            "qhd,khd->hqk", query, keys, preferred_element_type=jnp.float32
        ) / jnp.sqrt(jnp.float32(HD))
        attention_valid = jnp.arange(frames_count, dtype=jnp.int32) < length
        scores = jnp.where(attention_valid[None, None, :], scores, jnp.float32(-1e30))
        probs = jax.nn.softmax(scores, axis=-1).astype(jnp.bfloat16)
        context = jnp.einsum(
            "hqk,khd->qhd", probs, values, preferred_element_type=jnp.float32
        ).astype(jnp.bfloat16)
        context = context.reshape(frames_count, heads_local * HD)
        partial_out = jnp.dot(context, full_out, preferred_element_type=jnp.float32)
        attended = lax.psum(partial_out.astype(jnp.bfloat16), "mp").astype(jnp.float32)
        result = (layer_input.astype(jnp.float32) + attended).astype(jnp.bfloat16)
        if step >= 1:
            valid = frame_ids < lengths[step - 1]
            summed = jnp.sum(
                jnp.where(valid[:, None], result.astype(jnp.float32), jnp.float32(0.0)), axis=0
            )
            pooled_rows.append(summed / lengths[step - 1].astype(jnp.float32))
        if step < count_utt:
            received = passed_along(result, "section", 1)
    pooled = jnp.stack(pooled_rows, axis=0)
    pooled = broadcast(pooled, "section", 1)
    return jnp.dot(
        lax.all_gather(pooled, "dp", axis=0, tiled=True) - center,
        whitening,
        precision=lax.Precision.HIGHEST,
        preferred_element_type=jnp.float32,
    )


def solution(mesh):
    in_specs = (
        P("dp", None, None),
        P("dp"),
        P(None, "mp"),
        P("section", None),
        P("section", "dp", "mp"),
        P("section", "mp", "dp"),
        P(),
        P(None, "dp"),
    )
    out_specs = P(None, "dp")
    return jax.shard_map(body, mesh=mesh, in_specs=in_specs, out_specs=out_specs, check_vma=False)
```

profile of v0, /device:TPU:4, one launch (start us, length us, event | category | flops | bytes accessed | tf_op | source)
XLA Modules:
  0.0 596.0 jit_solution(13150222934486986474)
XLA Ops:
  6.5 0.0 copy-start
  6.5 0.0 all-gather.8.cloned.1.call-start
  6.5 1.5 copy.22
  8.0 0.0 all-gather.8.cloned.1.call-update
  8.0 0.0 all-gather.6.cloned.1.call-start
  8.1 1.7 copy.19
  9.8 0.0 all-gather.6.cloned.1.call-update
  9.8 0.0 all-reduce.3.cloned.1.call-start
  10.5 0.7 reduce
  11.3 0.0 copy-done
  11.3 1.2 convolution_convert_fusion.2
  12.5 16.5 %all_gather.13 = bf16[128,1920]{0,1:T(8,128)(2,1)S(1)} all-gather(bf16[128,480]{0,1:T(8,128)(2,1)S(1)} %convolution_convert_fusion.2), channel_id=1, replica_groups=mesh['dp'=64,'section'=2,'mp'=4] {'mp'}, dimensions={1}, use_global_device_ids=true | all-gather | bytes 614400 | tf_op jit(solution)/shard_map/all_gather | solution.py:50
  29.0 0.3 convert_reduce_fusion.1
  29.3 0.3 fusion.27
  29.6 131.5 %all-gather.8.cloned.1.call-done = bf16[1,480,1920]{1,0,2:T(2,128)(2,1)} async-done(((bf16[1,480,30]{1,0,2:T(2,128)(2,1)}), bf16[1,480,1920]{1,0,2:T(2,128)(2,1)}) %all-gather.8.cloned.1.call-update) | async-done | bytes 1843216 | tf_op jit(solution)/shard_map/all_gather | solution.py:39
  161.1 7.6 %copy.23 = bf16[1,480,1920]{2,1,0:T(8,128)(2,1)S(1)} copy(bf16[1,480,1920]{1,0,2:T(2,128)(2,1)} %all-gather.8.cloned.1.call-done) | data formatting | bytes 3686400 | tf_op jit(solution)/shard_map/all_gather | solution.py:39
  168.7 157.5 %all-gather.6.cloned.1.call-done = bf16[1,1920,1440]{2,0,1:T(2,128)(2,1)} async-done(((bf16[1,30,1440]{2,0,1:T(2,128)(2,1)}), bf16[1,1920,1440]{2,0,1:T(2,128)(2,1)}) %all-gather.6.cloned.1.call-update) | async-done | bytes 5529616 | tf_op jit(solution)/shard_map/all_gather | solution.py:38
  326.2 23.4 %copy.20 = bf16[1,1920,1440]{1,2,0:T(8,128)(2,1)} copy(bf16[1,1920,1440]{2,0,1:T(2,128)(2,1)} %all-gather.6.cloned.1.call-done) | data formatting | bytes 11059200 | tf_op jit(solution)/shard_map/all_gather | solution.py:38
  349.6 4.3 fusion.9
  353.8 0.3 fusion.54
  354.1 0.2 fusion.17
  354.4 0.9 convolution_convert_fusion.4
  355.3 2.6 convolution_convert_fusion.1
  357.9 0.0 all-reduce.3.cloned.1.call-update
  357.9 0.0 all-reduce.5.cloned.1.call-start
  357.9 52.0 %all-reduce.3.cloned.1.call-done = bf16[128,1920]{0,1:T(8,128)(2,1)} async-done(((bf16[128,1920]{0,1:T(8,128)(2,1)}), bf16[128,1920]{0,1:T(8,128)(2,1)}) %all-reduce.3.cloned.1.call-update) | async-done | bytes 491536 | tf_op jit(solution)/shard_map/psum | solution.py:71
  410.0 1.2 fusion.30
  411.2 1.3 collective-permute-start
  412.5 1.4 collective-permute-done
  413.9 0.3 convert_reduce_fusion
  414.2 0.3 fusion.24
  414.5 0.0 copy-start.2
  414.5 0.0 copy-start.3
  414.5 4.3 fusion.6
  418.8 0.0 copy-start.1
  418.8 0.7 copy-done.1
  419.6 0.3 fusion.55
  419.9 1.2 fusion.16
  421.1 1.1 convolution_convert_fusion.3
  422.2 1.7 convolution_convert_fusion
  423.9 0.0 all-reduce.5.cloned.1.call-update
  423.9 59.0 %all-reduce.5.cloned.1.call-done = bf16[128,1920]{0,1:T(8,128)(2,1)} async-done(((bf16[128,1920]{0,1:T(8,128)(2,1)}), bf16[128,1920]{0,1:T(8,128)(2,1)}) %all-reduce.5.cloned.1.call-update) | async-done | bytes 491536 | tf_op jit(solution)/shard_map/psum | solution.py:71
  483.0 1.4 select_reduce_fusion
  484.4 2.5 psum.23
  486.9 101.4 %all-gather.2 = f32[64,1,1920]{2,1,0:T(1,128)S(1)} all-gather(f32[1,1,1920]{2,1,0:T(1,128)S(1)} %bitcast.80), channel_id=1, replica_groups=mesh['dp'=64,'section'=2,'mp'=4] {'dp'}, dimensions={0}, use_global_device_ids=true | all-gather | bytes 499200 | tf_op jit(solution)/shard_map/all_gather | solution.py:84
  588.3 0.0 copy-done.2
  588.3 0.0 copy-done.3
  588.3 1.1 fusion.34
  (7 shorter events, 0.1 us)
Async XLA Ops:
  6.5 4.7 copy-start
  6.5 154.6 %all-gather.8.cloned.1.call-start = ((), (), s32[]{:S(2)}) async-start(), calls=%async_computation.3 | async-start | bytes 3993600 | tf_op jit(solution)/shard_map/all_gather | solution.py:39
  8.0 318.1 %all-gather.6.cloned.1.call-start = ((), (), s32[]{:S(2)}) async-start(), calls=%async_computation.2 | async-start | bytes 11980800 | tf_op jit(solution)/shard_map/all_gather | solution.py:38
  9.8 400.1 %all-reduce.3.cloned.1.call-start = ((), (), s32[]{:S(2)}) async-start(), calls=%async_computation | async-start | bytes 983040 | tf_op jit(solution)/shard_map/psum | solution.py:71
  357.9 125.1 %all-reduce.5.cloned.1.call-start = ((), (), s32[]{:S(2)}) async-start(), calls=%async_computation.1 | async-start | bytes 983040 | tf_op jit(solution)/shard_map/psum | solution.py:71
  411.2 2.8 collective-permute-start
  414.5 173.8 %copy-start.2 = (f32[1920,16]{0,1:T(8,128)S(1)}, f32[1920,16]{0,1:T(8,128)}, u32[]{:S(2)}) copy-start(f32[1920,16]{0,1:T(8,128)} %param.15) | copy-start | bytes 368644
  414.5 173.8 %copy-start.3 = (f32[1920]{0:T(1024)S(1)}, f32[1920]{0:T(1024)}, u32[]{:S(2)}) copy-start(f32[1920]{0:T(1024)} %param.14) | copy-start | bytes 23044
  418.8 0.7 copy-start.1
Sparse Core Ops, SparseCore 0:
  10.3 150.7 all-gather.7
  164.1 162.0 all-gather.5
  358.0 51.9 all-reduce.2
  424.1 58.8 all-reduce.4
where the time goes:
time: 597 us; the launch traced here: 596 us
  waiting for transfers between devices  402 us (67%)
  blocking collectives  120 us (20%)
  local copies, waits for them, and re-layouts  34.9 us (6%)
  matrix products  19.3 us (3%)
  between operations  13.9 us (2%)
    all_gather x1, waiting for transfers between devices, body(): lax.all_gather(qkv_local, 'dp', axis=0, tiled=True)  157 us
    all_gather x1, waiting for transfers between devices, body(): lax.all_gather(out_local, 'dp', axis=1, tiled=True)  132 us
    psum x2, waiting for transfers between devices, body(): lax.psum(partial_out.astype(jnp.bfloat16), 'mp').astype(jnp.float32)  111 us
    all_gather x1, blocking collectives, body(): lax.all_gather(pooled, 'dp', axis=0, tiled=True) - center  101 us
    all_gather x1, local copies, waits for them, and re-layouts, body(): lax.all_gather(qkv_local, 'dp', axis=0, tiled=True)  23.4 us
    all_gather x1, blocking collectives, body(): projected = lax.all_gather(projected_part, 'mp', axis=1, tiled=True)  16.5 us
  transfers between devices with their start and end apart: 5, of which 5 were waited for; matrix products, arithmetic and copies ran while one was open for 2% of the time, Pallas kernels for 0%

commit v1 on v0

--- a/solution.py
+++ b/solution.py
@@ -68,7 +68,9 @@
         ).astype(jnp.bfloat16)
         context = context.reshape(frames_count, heads_local * HD)
         partial_out = jnp.dot(context, full_out, preferred_element_type=jnp.float32)
-        attended = lax.psum(partial_out.astype(jnp.bfloat16), "mp").astype(jnp.float32)
+        attended = jnp.sum(lax.all_gather(partial_out.astype(jnp.bfloat16), "mp"), axis=0).astype(
+            jnp.float32
+        )
         result = (layer_input.astype(jnp.float32) + attended).astype(jnp.bfloat16)
         if step >= 1:
             valid = frame_ids < lengths[step - 1]

time: 597 us -> 559 us (0.936)
  the two profiles are of different devices: /device:TPU:4 before, /device:TPU:8 now
where the time goes in v1:
time: 559 us; the launch traced here: 557 us
  waiting for transfers between devices  364 us (65%)
  blocking collectives  116 us (21%)
  local copies, waits for them, and re-layouts  36.2 us (6%)
  matrix products  18.4 us (3%)
  between operations  13.9 us (2%)
  other arithmetic  7.14 us (1%)
    all_gather x1, waiting for transfers between devices, body(): lax.all_gather(qkv_local, 'dp', axis=0, tiled=True)  157 us
    all_gather x1, waiting for transfers between devices, body(): lax.all_gather(out_local, 'dp', axis=1, tiled=True)  134 us
    all_gather x1, blocking collectives, body(): lax.all_gather(pooled, 'dp', axis=0, tiled=True) - center  101 us
    all_gather x2, waiting for transfers between devices, body(): lax.all_gather(partial_out.astype(jnp.bfloat16), 'mp')  70.9 us
    all_gather x1, local copies, waits for them, and re-layouts, body(): lax.all_gather(qkv_local, 'dp', axis=0, tiled=True)  23.4 us
    all_gather x1, blocking collectives, body(): projected = lax.all_gather(projected_part, 'mp', axis=1, tiled=True)  13.1 us
  transfers between devices with their start and end apart: 5, of which 5 were waited for; matrix products, arithmetic and copies ran while one was open for 2% of the time, Pallas kernels for 0%

profile of v1, /device:TPU:8, one launch (start us, length us, event | category | flops | bytes accessed | tf_op | source)
XLA Modules:
  0.0 557.3 jit_solution(16892474857828097255)
XLA Ops:
  6.5 0.0 copy-start
  6.5 1.5 copy.20
  8.0 0.0 all-gather.12.cloned.1.call-update
  8.0 0.0 all-gather.10.cloned.1.call-start
  8.1 1.7 copy.17
  9.8 0.0 all-gather.10.cloned.1.call-update
  9.8 0.0 all-gather.14.cloned.1.call-start
  10.5 0.7 reduce.2
  11.3 1.2 convolution_convert_fusion.2
  12.5 13.1 %all_gather.25 = bf16[128,1920]{0,1:T(8,128)(2,1)S(1)} all-gather(bf16[128,480]{0,1:T(8,128)(2,1)S(1)} %convolution_convert_fusion.2), channel_id=1, replica_groups=mesh['dp'=64,'section'=2,'mp'=4] {'mp'}, dimensions={1}, use_global_device_ids=true | all-gather | bytes 614400 | tf_op jit(solution)/shard_map/all_gather | solution.py:50
  25.5 0.3 convert_reduce_fusion.1
  25.8 0.3 fusion.27
  26.1 133.6 %all-gather.12.cloned.1.call-done = bf16[1,480,1920]{1,0,2:T(2,128)(2,1)} async-done(((bf16[1,480,30]{1,0,2:T(2,128)(2,1)}), bf16[1,480,1920]{1,0,2:T(2,128)(2,1)}) %all-gather.12.cloned.1.call-update) | async-done | bytes 1843216 | tf_op jit(solution)/shard_map/all_gather | solution.py:39
  159.7 7.6 %copy.21 = bf16[1,480,1920]{2,1,0:T(8,128)(2,1)S(1)} copy(bf16[1,480,1920]{1,0,2:T(2,128)(2,1)} %all-gather.12.cloned.1.call-done) | data formatting | bytes 3686400 | tf_op jit(solution)/shard_map/all_gather | solution.py:39
  167.3 157.5 %all-gather.10.cloned.1.call-done = bf16[1,1920,1440]{2,0,1:T(2,128)(2,1)} async-done(((bf16[1,30,1440]{2,0,1:T(2,128)(2,1)}), bf16[1,1920,1440]{2,0,1:T(2,128)(2,1)}) %all-gather.10.cloned.1.call-update) | async-done | bytes 5529616 | tf_op jit(solution)/shard_map/all_gather | solution.py:38
  324.8 23.4 %copy.18 = bf16[1,1920,1440]{1,2,0:T(8,128)(2,1)} copy(bf16[1,1920,1440]{2,0,1:T(2,128)(2,1)} %all-gather.10.cloned.1.call-done) | data formatting | bytes 11059200 | tf_op jit(solution)/shard_map/all_gather | solution.py:38
  348.2 4.3 fusion.9
  352.5 0.3 fusion.54
  352.8 0.2 fusion.17
  353.0 0.9 convolution_convert_fusion.4
  353.9 2.2 convolution_convert_fusion.1
  356.1 0.0 all-gather.14.cloned.1.call-update
  356.1 0.0 all-gather.16.cloned.1.call-start
  356.2 33.2 %all-gather.14.cloned.1.call-done = bf16[512,1920]{1,0:T(8,128)(2,1)} async-done(((bf16[128,1920]{1,0:T(8,128)(2,1)}), bf16[512,1920]{1,0:T(8,128)(2,1)}) %all-gather.14.cloned.1.call-update) | async-done | bytes 1966096 | tf_op jit(solution)/shard_map/all_gather | solution.py:71
  389.4 1.9 reduce_sum.90
  391.3 1.0 copy.22
  392.3 1.2 fusion.30
  393.5 1.8 collective-permute-start
  395.2 1.4 collective-permute-done
  396.7 0.3 convert_reduce_fusion
  397.0 0.3 fusion.24
  397.3 4.3 fusion.6
  401.6 0.7 copy-done.1
  402.3 0.3 fusion.55
  402.6 1.2 fusion.16
  403.8 1.1 convolution_convert_fusion.3
  404.9 0.0 copy-start.2
  404.9 0.0 copy-start.3
  405.0 1.3 convolution_convert_fusion
  406.2 0.0 all-gather.16.cloned.1.call-update
  406.3 37.7 %all-gather.16.cloned.1.call-done = bf16[512,1920]{1,0:T(8,128)(2,1)} async-done(((bf16[128,1920]{1,0:T(8,128)(2,1)}), bf16[512,1920]{1,0:T(8,128)(2,1)}) %all-gather.16.cloned.1.call-update) | async-done | bytes 1966096 | tf_op jit(solution)/shard_map/all_gather | solution.py:71
  443.9 1.9 reduce_sum.94
  445.8 0.3 copy.24
  446.1 0.4 select_reduce_fusion
  446.5 2.5 psum.7
  449.0 100.6 %all-gather.4 = f32[64,1,1920]{2,1,0:T(1,128)S(1)} all-gather(f32[1,1,1920]{2,1,0:T(1,128)S(1)} %bitcast.84), channel_id=1, replica_groups=mesh['dp'=64,'section'=2,'mp'=4] {'dp'}, dimensions={0}, use_global_device_ids=true | all-gather | bytes 499200 | tf_op jit(solution)/shard_map/all_gather | solution.py:86
  549.6 0.0 copy-done.3
  549.6 1.1 fusion.34
  (11 shorter events, 0.1 us)
Async XLA Ops:
  6.5 4.7 copy-start
  6.5 153.2 %all-gather.12.cloned.1.call-start = ((), (), s32[]{:S(2)}) async-start(), calls=%async_computation.1 | async-start | bytes 3993600 | tf_op jit(solution)/shard_map/all_gather | solution.py:39
  8.0 316.8 %all-gather.10.cloned.1.call-start = ((), (), s32[]{:S(2)}) async-start(), calls=%async_computation | async-start | bytes 11980800 | tf_op jit(solution)/shard_map/all_gather | solution.py:38
  9.8 379.6 %all-gather.14.cloned.1.call-start = ((), (), s32[]{:S(2)}) async-start(), calls=%async_computation.2 | async-start | bytes 2457600 | tf_op jit(solution)/shard_map/all_gather | solution.py:71
  356.1 87.8 %all-gather.16.cloned.1.call-start = ((), (), s32[]{:S(2)}) async-start(), calls=%async_computation.3 | async-start | bytes 2457600 | tf_op jit(solution)/shard_map/all_gather | solution.py:71
  393.5 3.2 collective-permute-start
  401.5 0.7 copy-start.1
  404.9 144.7 %copy-start.2 = (f32[1920,16]{0,1:T(8,128)S(1)}, f32[1920,16]{0,1:T(8,128)}, u32[]{:S(2)}) copy-start(f32[1920,16]{0,1:T(8,128)} %param.15) | copy-start | bytes 368644
  404.9 144.7 %copy-start.3 = (f32[1920]{0:T(1024)S(1)}, f32[1920]{0:T(1024)}, u32[]{:S(2)}) copy-start(f32[1920]{0:T(1024)} %param.14) | copy-start | bytes 23044
Sparse Core Ops, SparseCore 0:
  10.3 149.3 all-gather.11
  162.7 162.1 all-gather.9
  356.3 33.1 all-gather.13
  406.4 37.5 all-gather.15
